TPU v7x, 256 devices: a whole 4x4x8 slice. The times are simulated.
256 devices in a mesh: grp: 32 (over y, z), head: 8 (over x, core).
Axes of the slice: x: 4, y: 4, z: 8, core: 2. Of those that a mesh axis runs over, the one named last changes fastest.
Arguments:
- long_queries: bfloat16 [32768, 64, 128], P(('grp', 'head')), may hold values from -24 to 24
- long_pairs: bfloat16 [32768, 8, 256], P(('grp', 'head')), may hold values from -24 to 24
- short_queries: bfloat16 [32768, 64, 128], P(('grp', 'head')), may hold values from -24 to 24
- short_pairs: bfloat16 [32768, 8, 256], P(('grp', 'head')), may hold values from -24 to 24
- doc_lengths: int32 [32, 32], replicated, may hold values from 1 to 64, 1024 in all within a row
- destinations: int32 [32, 32], replicated, may hold values from 0 to 31, each once within a row
Outputs:
- long_result: bfloat16 [32768, 8192], P(('grp', 'head'))
- short_placed: bfloat16 [65536, 8192], P('grp', 'head')
Inputs may be any that keep to these rules, and one draw needn't show every extreme that they name: `doc_lengths`: each row sums to 1024, and each row has a document of exactly 64 tokens. `destinations`: each row is a permutation, so every group receives exactly one short document from every group.
All inputs are finite; a program needn't handle non-finite values.
Results may differ from a plain program's by a relative error of at most 0.0047.
Values may be sent and summed in bfloat16 or wider, within the bound.
A program may use at most 128 MiB of HBM per device.

v0:
```python
import math

import jax
import jax.numpy as jnp
from jax import lax
from jax.sharding import PartitionSpec as P


def attend_rows(queries, pair_rows, allowed):
    row_count = queries.shape[0]
    pair_heads = pair_rows.shape[1]
    head_size = queries.shape[2]
    group_size = queries.shape[1] // pair_heads
    grouped = queries.reshape(row_count, pair_heads, group_size, head_size)
    key_part = pair_rows[:, :, :head_size]
    value_part = pair_rows[:, :, head_size:]
    score_scale = 1.0 / math.sqrt(head_size)
    scores = (
        jnp.einsum("qhgd,khd->hgqk", grouped, key_part, preferred_element_type=jnp.float32)
        * score_scale
    )
    scores = jnp.where(allowed[None, None], scores, -1e30)
    row_max = jnp.max(scores, axis=-1, keepdims=True)
    raised = jnp.exp(scores - row_max)
    weights = (raised / jnp.sum(raised, axis=-1, keepdims=True)).astype(jnp.bfloat16)
    head_mix = jnp.einsum("hgqk,khd->qhgd", weights, value_part, preferred_element_type=jnp.float32)
    return head_mix.reshape(row_count, queries.shape[1], head_size)


def doc_attend(queries, pair_rows, length):
    position = jnp.arange(queries.shape[0], dtype=jnp.int32)
    allowed = (position[None, :] <= position[:, None]) & (position[None, :] < length)
    head_mix = attend_rows(queries, pair_rows, allowed)
    valid_rows = (position < length)[:, None, None]
    return jnp.where(valid_rows, head_mix, 0.0).astype(jnp.bfloat16)


def on_device(long_queries, long_pairs, short_queries, short_pairs, doc_lengths, destinations):
    head_queries, head_pairs = (
        lax.all_to_all(long_queries, "head", split_axis=1, concat_axis=0, tiled=True),
        lax.all_to_all(long_pairs, "head", split_axis=1, concat_axis=0, tiled=True),
    )
    span_rows = head_queries.shape[0]
    block_rows = min(512, span_rows)
    pieces = []
    for first_row in range(0, span_rows, block_rows):
        last_row = first_row + block_rows
        query_pos = first_row + jnp.arange(block_rows, dtype=jnp.int32)
        key_pos = jnp.arange(last_row, dtype=jnp.int32)
        allowed = key_pos[None, :] <= query_pos[:, None]
        pieces.append(
            attend_rows(head_queries[first_row:last_row], head_pairs[:last_row], allowed).astype(
                jnp.bfloat16
            )
        )
    head_mix = jnp.concatenate(pieces, axis=0)
    returned = lax.all_to_all(head_mix, "head", split_axis=0, concat_axis=1, tiled=True)
    long_result = returned.reshape(returned.shape[0], -1)
    group_count = lax.axis_size("grp")
    local_rows = short_queries.shape[0]
    doc_span = 2 * local_rows * lax.axis_size("head") // group_count
    own_group = lax.axis_index("grp")
    own_lengths = lax.dynamic_index_in_dim(doc_lengths, own_group, 0, keepdims=False)
    own_targets = lax.dynamic_index_in_dim(destinations, own_group, 0, keepdims=False)
    starts = jnp.cumsum(own_lengths) - own_lengths
    slot_ids = jnp.arange(group_count, dtype=jnp.int32)
    chosen = (own_targets[None, :] == slot_ids[:, None]).astype(jnp.int32)
    slot_length = jnp.sum(chosen * own_lengths[None, :], axis=1)
    slot_start = jnp.sum(chosen * starts[None, :], axis=1)
    position = jnp.arange(doc_span, dtype=jnp.int32)
    valid_rows = position[None, :] < slot_length[:, None]
    row_index = jnp.where(valid_rows, slot_start[:, None] + position[None, :], 0)
    group_queries, group_pairs = (
        lax.all_to_all(short_queries, "head", split_axis=1, concat_axis=0, tiled=True),
        lax.all_to_all(short_pairs, "head", split_axis=1, concat_axis=0, tiled=True),
    )
    slot_queries = group_queries[row_index]
    slot_pairs = group_pairs[row_index]
    got_queries, got_pairs = (
        lax.all_to_all(slot_queries, "grp", split_axis=0, concat_axis=0, tiled=True),
        lax.all_to_all(slot_pairs, "grp", split_axis=0, concat_axis=0, tiled=True),
    )
    arriving = (destinations == own_group).astype(jnp.int32)
    got_lengths = jnp.sum(arriving * doc_lengths, axis=1)
    placed = jax.vmap(doc_attend)(got_queries, got_pairs, got_lengths)
    short_placed = placed.reshape(placed.shape[0] * placed.shape[1], -1)
    return (long_result, short_placed)


def solution(mesh):
    placed = (
        P(("grp", "head"), None, None),
        P(("grp", "head"), None, None),
        P(("grp", "head"), None, None),
        P(("grp", "head"), None, None),
        P(),
        P(),
    )
    return jax.shard_map(
        on_device,
        mesh=mesh,
        in_specs=placed,
        out_specs=(P(("grp", "head"), None), P("grp", "head")),
        check_vma=False,
    )
```

profile of v0, /device:TPU:6, one launch (start us, length us, event | category | flops | bytes accessed | tf_op | source)
XLA Modules:
  0.0 293.6 jit_solution(1412407909209046950)
XLA Ops:
  0.6 0.0 copy-start.5
  0.6 0.0 copy-start.6
  0.7 1.9 copy.37
  2.6 5.6 %all-to-all-start = ((bf16[128,8,256]{2,0,1:T(8,128)(2,1)}), bf16[128,8,256]{2,0,1:T(8,128)(2,1)S(1)}, u32[]{:S(2)}, u32[]{:S(2)}) async-start(bf16[128,8,256]{2,0,1:T(8,128)(2,1)} %copy.37), calls=%async_computation | async-start | bytes 1048576 | tf_op jit(solution)/shard_map/all_to_all | solution.py:41
  8.2 1.9 copy.44
  10.2 6.3 %all-to-all-done = bf16[128,8,256]{2,0,1:T(8,128)(2,1)S(1)} async-done(((bf16[128,8,256]{2,0,1:T(8,128)(2,1)}), bf16[128,8,256]{2,0,1:T(8,128)(2,1)S(1)}, u32[]{:S(2)}, u32[]{:S(2)}) %all-to-all-start) | async-done | bytes 524320 | tf_op jit(solution)/shard_map/all_to_all | solution.py:41
  16.4 0.0 copy-start.1
  16.4 0.8 copy-done.1
  17.2 5.5 %all-to-all-start.3 = ((bf16[128,8,256]{2,0,1:T(8,128)(2,1)}), bf16[128,8,256]{2,0,1:T(8,128)(2,1)S(1)}, u32[]{:S(2)}, u32[]{:S(2)}) async-start(bf16[128,8,256]{2,0,1:T(8,128)(2,1)} %copy.44), calls=%async_computation.3 | async-start | bytes 1048576 | tf_op jit(solution)/shard_map/all_to_all | solution.py:75
  22.7 4.3 %copy.38 = bf16[128,64,128]{2,0,1:T(8,128)(2,1)} copy(bf16[128,64,128]{2,1,0:T(8,128)(2,1)} %param.6) | data formatting | bytes 4194304 | tf_op args[0]
  27.0 4.0 %all-to-all-done.3 = bf16[128,8,256]{2,0,1:T(8,128)(2,1)S(1)} async-done(((bf16[128,8,256]{2,0,1:T(8,128)(2,1)}), bf16[128,8,256]{2,0,1:T(8,128)(2,1)S(1)}, u32[]{:S(2)}, u32[]{:S(2)}) %all-to-all-start.3) | async-done | bytes 524320 | tf_op jit(solution)/shard_map/all_to_all | solution.py:75
  31.0 5.6 %all-to-all-start.1 = ((bf16[128,64,128]{2,0,1:T(8,128)(2,1)}), bf16[128,64,128]{2,0,1:T(8,128)(2,1)S(1)}, u32[]{:S(2)}, u32[]{:S(2)}) async-start(bf16[128,64,128]{2,0,1:T(8,128)(2,1)} %copy.38), calls=%async_computation.1 | async-start | bytes 4194304 | tf_op jit(solution)/shard_map/all_to_all | solution.py:40
  36.6 4.3 %copy.48 = bf16[128,64,128]{2,0,1:T(8,128)(2,1)} copy(bf16[128,64,128]{2,1,0:T(8,128)(2,1)} %param.8) | data formatting | bytes 4194304 | tf_op args[2]
  40.9 0.0 copy-done.5
  40.9 0.2 reduce-window_clone.1
  41.1 0.0 copy-done.6
  41.1 0.1 select_reduce_fusion.1
  41.2 0.1 compare_select_fusion
  41.3 0.1 reshape.299
  41.4 0.1 iota_compare_fusion.1
  41.5 0.4 iota_compare_fusion
  41.9 1.7 slice.46
  43.5 9.0 %gather_fusion = bf16[2048,256]{1,0:T(8,128)(2,1)} fusion(bf16[1024,256]{1,0:T(8,128)(2,1)S(1)} %bitcast.175, s32[2048]{0:T(1024)S(1)} %broadcast_clamp_fusion), kind=kCustom, calls=%fused_computation | custom fusion | bytes 2105344 | tf_op jit(solution)/shard_map/gather | solution.py:78
  52.5 0.0 copy-start.2
  52.5 9.2 %all-to-all-done.1 = bf16[128,64,128]{2,0,1:T(8,128)(2,1)S(1)} async-done(((bf16[128,64,128]{2,0,1:T(8,128)(2,1)}), bf16[128,64,128]{2,0,1:T(8,128)(2,1)S(1)}, u32[]{:S(2)}, u32[]{:S(2)}) %all-to-all-start.1) | async-done | bytes 2097184 | tf_op jit(solution)/shard_map/all_to_all | solution.py:40
  61.7 6.7 %all-to-all-start.5 = ((bf16[128,64,128]{2,0,1:T(8,128)(2,1)}), bf16[128,64,128]{2,0,1:T(8,128)(2,1)}, u32[]{:S(2)}, u32[]{:S(2)}) async-start(bf16[128,64,128]{2,0,1:T(8,128)(2,1)} %copy.48), calls=%async_computation.5 | async-start | bytes 4194304 | tf_op jit(solution)/shard_map/all_to_all | solution.py:74
  68.4 0.1 copy.66
  68.5 0.2 fusion.42
  68.7 0.0 copy-done.2
  68.7 7.3 %fusion.1 = (f32[8,512]{1,0:T(8,128)S(1)}, f32[1024,512,8]{1,0,2:T(8,128)}) fusion(pred[512,1024]{0,1:T(8,128)(4,1)S(1)} %iota_compare_fusion, bf16[512,8,128]{2,0,1:T(8,128)(2,1)S(1)} %bitcast.182, bf16[1024,1,256]{2,0,1:T(8,128)(2,1)S(1)} %bitcast.187), kind=kOutput, calls=%fused_computation.6 | convolution fusion | flops 1086320640 | bytes 18628608 | tf_op jit(solution)/shard_map/qhgd,khd->hgqk/dot_general | solution.py:19
  76.0 0.0 copy-start.3
  76.0 9.2 %fusion = f32[8,512]{1,0:T(8,128)S(1)} fusion(f32[1024,512,8]{1,0,2:T(8,128)} %get-tuple-element.7, f32[8,512]{1,0:T(8,128)S(1)} %get-tuple-element.6, pred[512,1024]{0,1:T(8,128)(4,1)S(1)} %iota_compare_fusion), kind=kLoop, calls=%fused_computation.5 | loop fusion | flops 16773120 | bytes 17334272 | tf_op jit(solution)/shard_map/reduce_sum | solution.py:25
  85.2 0.0 copy-done.3
  85.2 4.7 %fusion.7 = (f32[8,512]{1,0:T(8,128)S(1)}, f32[512,512,8]{1,0,2:T(8,128)}) fusion(pred[512,512]{0,1:T(8,128)(4,1)S(1)} %iota_compare_fusion.1, bf16[512,8,128]{2,0,1:T(8,128)(2,1)S(1)} %bitcast.183, bf16[512,1,256]{2,0,1:T(8,128)(2,1)S(1)} %bitcast.190), kind=kOutput, calls=%fused_computation.19 | convolution fusion | flops 543158272 | bytes 9846784 | tf_op jit(solution)/shard_map/qhgd,khd->hgqk/dot_general | solution.py:19
  89.9 8.3 %fusion.27 = bf16[512,8,128]{2,0,1:T(8,128)(2,1)S(1)} fusion(f32[8,512]{1,0:T(8,128)S(1)} %fusion, f32[8,512]{1,0:T(8,128)S(1)} %get-tuple-element.6, f32[1024,512,8]{1,0,2:T(8,128)} %get-tuple-element.7, pred[512,1024]{0,1:T(8,128)(4,1)S(1)} %iota_compare_fusion, bf16[1024,1,256]{2,0,1:T(8,128)(2,1)S(1)} %bitcast.188), kind=kOutput, calls=%fused_computation.37 | convolution fusion | flops 1095237632 | bytes 18644992 | tf_op jit(solution)/shard_map/hgqk,khd->qhgd/dot_general | solution.py:26
  98.2 0.0 copy-start.4
  98.3 0.0 all-to-all-done.5
  98.3 11.3 %all-to-all-start.4 = ((bf16[32,64,1,256]{3,1,2,0:T(8,128)(2,1)}), bf16[32,64,1,256]{3,1,2,0:T(8,128)(2,1)S(1)}, u32[]{:S(2)}, u32[]{:S(2)}) async-start(bf16[32,64,1,256]{3,1,2,0:T(8,128)(2,1)} %bitcast.41), calls=%async_computation.4 | async-start | bytes 2097152 | tf_op jit(solution)/shard_map/all_to_all | solution.py:81
  109.6 0.0 copy-start
  109.6 5.3 %fusion.5 = f32[8,512]{1,0:T(8,128)S(1)} fusion(f32[512,512,8]{1,0,2:T(8,128)} %get-tuple-element.9, f32[8,512]{1,0:T(8,128)S(1)} %get-tuple-element.8, pred[512,512]{0,1:T(8,128)(4,1)S(1)} %iota_compare_fusion.1), kind=kLoop, calls=%fused_computation.17 | loop fusion | flops 8384512 | bytes 8683520 | tf_op jit(solution)/shard_map/reduce_sum | solution.py:25
  114.9 0.0 copy-done.4
  114.9 0.5 copy-done
  115.4 3.3 %fusion.30 = bf16[512,8,128]{2,0,1:T(8,128)(2,1)S(1)} fusion(f32[8,512]{1,0:T(8,128)S(1)} %fusion.5, f32[8,512]{1,0:T(8,128)S(1)} %get-tuple-element.8, f32[512,512,8]{1,0,2:T(8,128)S(1)} %copy-done, pred[512,512]{0,1:T(8,128)(4,1)S(1)} %iota_compare_fusion.1, bf16[512,1,256]{2,0,1:T(8,128)(2,1)S(1)} %bitcast.191), kind=kOutput, calls=%fused_computation.38 | convolution fusion | flops 547880960 | bytes 9863168 | tf_op jit(solution)/shard_map/hgqk,khd->qhgd/dot_general | solution.py:26
  118.6 0.1 pad_maximum_fusion
  118.8 2.7 copy.42
  121.5 17.0 %all-to-all-done.4 = bf16[32,64,1,256]{3,1,2,0:T(8,128)(2,1)S(1)} async-done(((bf16[32,64,1,256]{3,1,2,0:T(8,128)(2,1)}), bf16[32,64,1,256]{3,1,2,0:T(8,128)(2,1)S(1)}, u32[]{:S(2)}, u32[]{:S(2)}) %all-to-all-start.4) | async-done | bytes 1048608 | tf_op jit(solution)/shard_map/all_to_all | solution.py:81
  138.5 4.8 %all-to-all-start.2 = ((bf16[1024,8,128]{2,1,0:T(8,128)(2,1)}), bf16[1024,8,128]{2,1,0:T(8,128)(2,1)}, u32[]{:S(2)}, u32[]{:S(2)}) async-start(bf16[1024,8,128]{2,1,0:T(8,128)(2,1)} %copy.42), calls=%async_computation.2 | async-start | bytes 4194304 | tf_op jit(solution)/shard_map/all_to_all | solution.py:57
  143.3 3.0 %copy.50 = bf16[8,128,8,128]{3,2,1,0:T(8,128)(2,1)S(1)} copy(bf16[8,128,8,128]{3,1,2,0:T(8,128)(2,1)} %bitcast.52) | data formatting | bytes 4194304 | tf_op jit(solution)/shard_map/all_to_all | solution.py:74
  146.2 14.6 %gather_fusion.1 = bf16[2048,8,128]{2,1,0:T(8,128)(2,1)} fusion(bf16[1024,8,128]{2,1,0:T(8,128)(2,1)S(1)} %bitcast.176, s32[2048]{0:T(1024)S(1)} %broadcast_clamp_fusion), kind=kCustom, calls=%fused_computation.1 | custom fusion | bytes 8396800 | tf_op jit(solution)/shard_map/gather | solution.py:77
  160.8 5.4 %copy.51 = bf16[32,64,8,128]{3,1,2,0:T(8,128)(2,1)} copy(bf16[32,64,8,128]{3,2,1,0:T(8,128)(2,1)} %bitcast.178) | data formatting | bytes 8388608 | tf_op jit(solution)/shard_map/gather | solution.py:77
  166.2 2.3 all-to-all-done.2
  168.5 5.4 %all-to-all-start.6 = ((bf16[32,64,8,128]{3,1,2,0:T(8,128)(2,1)}), bf16[32,64,8,128]{3,1,2,0:T(8,128)(2,1)}, u32[]{:S(2)}, u32[]{:S(2)}) async-start(bf16[32,64,8,128]{3,1,2,0:T(8,128)(2,1)} %copy.51), calls=%async_computation.6 | async-start | bytes 8388608 | tf_op jit(solution)/shard_map/all_to_all | solution.py:80
  173.9 0.1 select_reduce_fusion.2
  174.0 0.1 iota_compare_fusion.5
  174.1 0.1 lt.73
  174.2 0.3 broadcast_and_fusion
  174.5 2.2 copy.43
  176.7 3.1 %copy.65 = bf16[16,8,64,128]{3,1,2,0:T(8,128)(2,1)} copy(bf16[16,8,64,128]{3,2,1,0:T(8,128)(2,1)S(1)} %bitcast.181) | data formatting | bytes 4194304
  179.8 90.8 %all-to-all-done.6 = bf16[32,64,8,128]{3,1,2,0:T(8,128)(2,1)} async-done(((bf16[32,64,8,128]{3,1,2,0:T(8,128)(2,1)}), bf16[32,64,8,128]{3,1,2,0:T(8,128)(2,1)}, u32[]{:S(2)}, u32[]{:S(2)}) %all-to-all-start.6) | async-done | bytes 4194336 | tf_op jit(solution)/shard_map/all_to_all | solution.py:80
  270.6 6.3 %fusion.8 = (f32[32,8,64]{2,1,0:T(8,128)S(1)}, f32[32,64,64,8]{2,1,3,0:T(8,128)S(1)}) fusion(pred[32,64,64]{1,2,0:T(8,128)(4,1)S(1)} %broadcast_and_fusion, bf16[32,64,8,128]{3,1,2,0:T(8,128)(2,1)} %all-to-all-done.6, bf16[32,64,1,256]{3,1,0,2:T(8,128)(2,1)S(1)} %bitcast.184), kind=kOutput, calls=%fused_computation.20 | convolution fusion | flops 271564800 | bytes 9240576 | tf_op jit(solution)/shard_map/vmap(qhgd,khd->hgqk)/dot_general | solution.py:19
  276.9 2.8 fusion.6
  279.7 3.1 %fusion.18 = bf16[32,64,1,8,128]{4,1,3,0,2:T(8,128)(2,1)S(1)} fusion(f32[32,8,64]{2,1,0:T(8,128)S(1)} %fusion.6, f32[32,64,64,8]{2,1,3,0:T(8,128)S(1)} %get-tuple-element.11, f32[32,8,64]{2,1,0:T(8,128)S(1)} %get-tuple-element.10, pred[32,64,64]{1,2,0:T(8,128)(4,1)S(1)} %broadcast_and_fusion, bf16[32,64,1,256]{3,1,0,2:T(8,128)(2,1)S(1)} %bitcast.185), kind=kOutput, calls=%fused_computation.30 | convolution fusion | flops 273678336 | bytes 13631488 | tf_op jit(solution)/shard_map/vmap(hgqk,khd->qhgd)/dot_general | solution.py:26
  282.8 8.1 %copy.53 = bf16[32,64,1,8,128]{4,3,1,0,2:T(8,128)(2,1)S(1)} copy(bf16[32,64,1,8,128]{4,1,3,0,2:T(8,128)(2,1)S(1)} %fusion.18) | data formatting | bytes 8388608 | tf_op jit(solution)/shard_map/vmap(hgqk,khd->qhgd)/transpose | solution.py:26
  290.9 2.5 fusion.2
  (6 shorter events, 0.0 us)
Async XLA Ops:
  0.6 40.2 %copy-start.5 = (s32[32,32]{1,0:T(8,128)S(1)}, s32[32,32]{1,0:T(8,128)}, u32[]{:S(2)}) copy-start(s32[32,32]{1,0:T(8,128)} %param.10) | copy-start | bytes 12292
  0.6 40.5 %copy-start.6 = (s32[32,32]{1,0:T(8,128)S(1)}, s32[32,32]{1,0:T(8,128)}, u32[]{:S(2)}) copy-start(s32[32,32]{1,0:T(8,128)} %param.11) | copy-start | bytes 12292
  2.6 13.8 %all-to-all-start = ((bf16[128,8,256]{2,0,1:T(8,128)(2,1)}), bf16[128,8,256]{2,0,1:T(8,128)(2,1)S(1)}, u32[]{:S(2)}, u32[]{:S(2)}) async-start(bf16[128,8,256]{2,0,1:T(8,128)(2,1)} %copy.37), calls=%async_computation | async-start | bytes 1048576 | tf_op jit(solution)/shard_map/all_to_all | solution.py:41
  16.4 0.8 copy-start.1
  17.2 13.7 %all-to-all-start.3 = ((bf16[128,8,256]{2,0,1:T(8,128)(2,1)}), bf16[128,8,256]{2,0,1:T(8,128)(2,1)S(1)}, u32[]{:S(2)}, u32[]{:S(2)}) async-start(bf16[128,8,256]{2,0,1:T(8,128)(2,1)} %copy.44), calls=%async_computation.3 | async-start | bytes 1048576 | tf_op jit(solution)/shard_map/all_to_all | solution.py:75
  31.0 30.7 %all-to-all-start.1 = ((bf16[128,64,128]{2,0,1:T(8,128)(2,1)}), bf16[128,64,128]{2,0,1:T(8,128)(2,1)S(1)}, u32[]{:S(2)}, u32[]{:S(2)}) async-start(bf16[128,64,128]{2,0,1:T(8,128)(2,1)} %copy.38), calls=%async_computation.1 | async-start | bytes 4194304 | tf_op jit(solution)/shard_map/all_to_all | solution.py:40
  52.5 16.2 %copy-start.2 = (bf16[128,8,256]{2,0,1:T(8,128)(2,1)S(1)}, bf16[128,8,256]{2,0,1:T(8,128)(2,1)}, u32[]{:S(2)}) copy-start(bf16[128,8,256]{2,0,1:T(8,128)(2,1)} %copy-done.1) | copy-start | bytes 1572868
  61.7 36.6 %all-to-all-start.5 = ((bf16[128,64,128]{2,0,1:T(8,128)(2,1)}), bf16[128,64,128]{2,0,1:T(8,128)(2,1)}, u32[]{:S(2)}, u32[]{:S(2)}) async-start(bf16[128,64,128]{2,0,1:T(8,128)(2,1)} %copy.48), calls=%async_computation.5 | async-start | bytes 4194304 | tf_op jit(solution)/shard_map/all_to_all | solution.py:74
  76.0 9.2 %copy-start.3 = (bf16[4,128,1,256]{3,1,0,2:T(8,128)(2,1)S(1)}, bf16[4,128,1,256]{3,1,0,2:T(8,128)(2,1)}, u32[]{:S(2)}) copy-start(bf16[4,128,1,256]{3,1,0,2:T(8,128)(2,1)} %slice.46) | copy-start | bytes 786436
  98.2 16.6 %copy-start.4 = (bf16[4,128,1,256]{3,1,0,2:T(8,128)(2,1)S(1)}, bf16[4,128,1,256]{3,1,0,2:T(8,128)(2,1)}, u32[]{:S(2)}) copy-start(bf16[4,128,1,256]{3,1,0,2:T(8,128)(2,1)} %slice.46) | copy-start | bytes 786436
  98.3 40.2 %all-to-all-start.4 = ((bf16[32,64,1,256]{3,1,2,0:T(8,128)(2,1)}), bf16[32,64,1,256]{3,1,2,0:T(8,128)(2,1)S(1)}, u32[]{:S(2)}, u32[]{:S(2)}) async-start(bf16[32,64,1,256]{3,1,2,0:T(8,128)(2,1)} %bitcast.41), calls=%async_computation.4 | async-start | bytes 2097152 | tf_op jit(solution)/shard_map/all_to_all | solution.py:81
  109.6 5.8 %copy-start = (f32[512,512,8]{1,0,2:T(8,128)S(1)}, f32[512,512,8]{1,0,2:T(8,128)}, u32[]{:S(2)}) copy-start(f32[512,512,8]{1,0,2:T(8,128)} %get-tuple-element.9) | copy-start | bytes 25165828
  138.5 30.0 %all-to-all-start.2 = ((bf16[1024,8,128]{2,1,0:T(8,128)(2,1)}), bf16[1024,8,128]{2,1,0:T(8,128)(2,1)}, u32[]{:S(2)}, u32[]{:S(2)}) async-start(bf16[1024,8,128]{2,1,0:T(8,128)(2,1)} %copy.42), calls=%async_computation.2 | async-start | bytes 4194304 | tf_op jit(solution)/shard_map/all_to_all | solution.py:57
  168.5 102.1 %all-to-all-start.6 = ((bf16[32,64,8,128]{3,1,2,0:T(8,128)(2,1)}), bf16[32,64,8,128]{3,1,2,0:T(8,128)(2,1)}, u32[]{:S(2)}, u32[]{:S(2)}) async-start(bf16[32,64,8,128]{3,1,2,0:T(8,128)(2,1)} %copy.51), calls=%async_computation.6 | async-start | bytes 8388608 | tf_op jit(solution)/shard_map/all_to_all | solution.py:80
where the time goes:
time: 299 us; the launch traced here: 294 us
  waiting for transfers between devices  130 us (43%)
  local copies, waits for them, and re-layouts  63.8 us (21%)
  starting transfers between devices  45 us (15%)
  matrix products  32.9 us (11%)
  other arithmetic  21.3 us (7%)
    all_to_all x1, waiting for transfers between devices, on_device(): lax.all_to_all(slot_queries, 'grp', split_axis=0, concat_axis=0, tiled=True)  90.8 us
    gather x2, local copies, waits for them, and re-layouts, on_device(): slot_queries = group_queries[row_index]  19.9 us
    dot_general x3, matrix products, attend_rows(): jnp.einsum('qhgd,khd->hgqk', grouped, key_part, preferred_element_type=jn...  18.3 us
    reduce_sum x3, other arithmetic, attend_rows(): jnp.sum(raised, axis=-1, keepdims=True)  17.2 us
    all_to_all x1, waiting for transfers between devices, on_device(): lax.all_to_all(slot_pairs, 'grp', split_axis=0, concat_axis=0, tiled=True)  17 us
    unnamed x19, local copies, waits for them, and re-layouts  16.8 us
    dot_general x3, matrix products, attend_rows(): jnp.einsum('hgqk,khd->qhgd', weights, value_part, preferred_element_type=...  14.6 us
    all_to_all x1, starting transfers between devices, on_device(): lax.all_to_all(slot_pairs, 'grp', split_axis=0, concat_axis=0, tiled=True)  11.3 us
  transfers between devices with their start and end apart: 7, of which 6 were waited for; matrix products, arithmetic and copies ran while one was open for 31% of the time, Pallas kernels for 0%

commit v1 on v0

v1 whole, which is shorter than its diff:
```python
import functools
import math

import jax
import jax.numpy as jnp
from jax import lax
from jax.experimental import pallas as pl
from jax.experimental.pallas import tpu as pltpu
from jax.sharding import PartitionSpec as P

MESH = pl.DeviceIdType.MESH
BF16 = jnp.bfloat16
F32 = jnp.float32

NG = 32
NH = 8
TOK = 128
QH = 8
D = 128
DOC = 64
TB = 16
NB = DOC // TB
WROWS = TB * NB * (NB + 1) // 2
SLOT = WROWS + DOC
KROWS = DOC + TB
SCALE2 = math.log2(math.e) / math.sqrt(D)


def wrow(block):
    return TB * block * (block + 1) // 2


def perm_matrix():
    row = lax.broadcasted_iota(jnp.int32, (D, D), 0)
    col = lax.broadcasted_iota(jnp.int32, (D, D), 1)
    return (col == (row % QH) * TB + row // QH).astype(BF16)


def slot_weights(q, k, length, perm):
    st = lax.dot_general(k, q, (((1,), (1,)), ((), ())), preferred_element_type=F32)
    out = []
    for b in range(NB):
        keys = TB * (b + 1)
        s = st[:keys, b * D : (b + 1) * D]
        key = lax.broadcasted_iota(jnp.int32, (keys, D), 0)
        tok = TB * b + lax.broadcasted_iota(jnp.int32, (keys, D), 1) // QH
        s = jnp.where(key <= tok, s, -1e30)
        top = jnp.max(s, axis=0, keepdims=True)
        p = jnp.exp2((s - top) * SCALE2)
        inv = 1.0 / jnp.sum(p, axis=0, keepdims=True)
        inv = jnp.where(tok[:1] < length, inv, 0.0)
        w = (p * inv).astype(BF16)
        w = jnp.dot(w, perm, preferred_element_type=F32).astype(BF16)
        out.append(w)
    return out


def main_kernel(
    sq, skv, lq, lkv, tabs,
    recv_out, long_out,
    gq, gkv, send, lall, lqv, lout, otile,
    xq_send, xq_recv, xk_send, xk_recv, z_send, z_recv,
    l_send, l_recv, f_send, f_recv, loc_sem,
):
    g = lax.axis_index("grp")
    h = lax.axis_index("head")
    y, z = g // 8, g % 8
    x, core = h // 2, h % 2

    def group_at(i):
        m = i % 8
        oz = jnp.where(m % 2 == 0, m // 2 + 1, 8 - (m // 2 + 1))
        oz = jnp.where(m == 7, 0, oz)
        oy = i // 8
        return ((y + oy) % 4) * 8 + (z + oz) % 8, ((y + 4 - oy) % 4) * 8 + (z + 8 - oz) % 8

    SELF = 7

    barrier = pltpu.get_barrier_semaphore()
    for o in range(1, NH):
        pl.semaphore_signal(barrier, inc=1, device_id=(g, (h + o) % NH), device_id_type=MESH)

    @pl.loop(1, NG)
    def _(o):
        pl.semaphore_signal(barrier, inc=1, device_id=((g + o) % NG, h), device_id_type=MESH)

    own = pl.ds(pl.multiple_of(h * TOK, TOK), TOK)
    own_kv = pl.ds(h * (TOK // TB), TOK // TB)
    own_q = pltpu.make_async_copy(sq.at[:, h], gq.at[own], loc_sem.at[0])
    own_k = pltpu.make_async_copy(skv.at[h], gkv.at[own_kv], loc_sem.at[1])
    own_lq = pltpu.make_async_copy(lq, lqv, loc_sem.at[2])
    own_lk = pltpu.make_async_copy(lkv, lall.at[h], loc_sem.at[3])
    own_q.start()
    own_k.start()
    own_lq.start()
    own_lk.start()
    pl.semaphore_wait(barrier, NH - 1 + NG - 1)

    def x_copies(o):
        peer = (h + o) % NH
        return (
            pltpu.make_async_remote_copy(
                skv.at[peer], gkv.at[own_kv], xk_send.at[o], xk_recv.at[o],
                device_id=(g, peer), device_id_type=MESH),
            pltpu.make_async_remote_copy(
                sq.at[:, peer], gq.at[own], xq_send.at[o], xq_recv.at[o],
                device_id=(g, peer), device_id_type=MESH),
        )

    for o in range(1, NH):
        for copy in x_copies(o):
            copy.start()

    gq[NH * TOK :, :, :] = jnp.zeros((DOC, QH, D), BF16)
    gkv[NH * TOK // TB :] = jnp.zeros((KROWS // TB, TB, 2 * D), BF16)

    own_q.wait()
    own_k.wait()
    for o in range(1, NH):
        for copy in x_copies(o):
            copy.wait_recv()
    for o in range(1, NH):
        for copy in x_copies(o):
            copy.wait_send()

    own_lk.wait()
    partner = h + 1 - 2 * core

    def l_copy(n):
        return pltpu.make_async_remote_copy(
            lkv, lall.at[h], l_send.at[n], l_recv.at[n],
            device_id=(g, (h + 2 * n) % NH), device_id_type=MESH)

    def f_copy(n):
        src = (h + NH - 2 * n) % NH
        return pltpu.make_async_remote_copy(
            lall.at[src], lall.at[src], f_send.at[n], f_recv.at[n],
            device_id=(g, partner), device_id_type=MESH)

    l_pair = pltpu.make_async_remote_copy(
        lkv, lall.at[h], f_send.at[0], f_recv.at[0],
        device_id=(g, partner), device_id_type=MESH)
    l_pair.start()
    for n in range(1, 4):
        @pl.when(x + n < 4)
        def _(n=n):
            l_copy(n).start()

    perm = perm_matrix()

    def z_copy(i):
        to, _ = group_at(i)
        return pltpu.make_async_remote_copy(
            send.at[i], recv_out.at[g], z_send.at[i], z_recv.at[i],
            device_id=(to, h), device_id_type=MESH)

    def slot(i):
        to, _ = group_at(i)
        length = tabs[1, to]
        shift = tabs[3, to]
        q = gq[pl.ds(tabs[0, to], DOC)].astype(F32).reshape(DOC * QH, D).astype(BF16)
        kv = gkv[pl.ds(tabs[2, to], KROWS // TB)].reshape(KROWS, 2 * D)
        pick = lax.broadcasted_iota(jnp.int32, (DOC, KROWS), 0) + shift
        pick = (pick == lax.broadcasted_iota(jnp.int32, (DOC, KROWS), 1)).astype(BF16)
        kv = jnp.dot(pick, kv, preferred_element_type=F32).astype(BF16)
        k, v = kv[:, :D], kv[:, D:]
        for b, w in enumerate(slot_weights(q, k, length, perm)):
            send[i, wrow(b) : wrow(b + 1), :] = w
        send[i, WROWS:SLOT, :] = v

    own_slot = pltpu.make_async_copy(send.at[SELF], recv_out.at[g], loc_sem.at[4])

    def send_slot(i):
        @pl.when(i != SELF)
        def _():
            z_copy(i).start()

        @pl.when(i == SELF)
        def _():
            own_slot.start()

    slot(0)

    @pl.loop(1, NG)
    def _(i):
        slot(i)
        send_slot(i - 1)

    send_slot(NG - 1)

    own_lq.wait()
    for n in range(1, 4):
        @pl.when(x >= n)
        def _(n=n):
            l_copy(n).wait_recv()
            f_copy(n).start()

    l_pair.wait_recv()
    for n in range(1, 4):
        @pl.when(x >= n)
        def _(n=n):
            f_copy(n).wait_recv()

    def long_tile(i, chips):
        c, t = i // 4, i % 4
        q = lqv[pl.ds(t * 32, 32), c].astype(F32).reshape(32 * QH, D).astype(BF16)
        scores = []
        for b in range(chips + 1):
            k = lall[2 * b : 2 * b + 2, c, :, 0:D].reshape(2 * TOK, D)
            scores.append(lax.dot_general(q, k, (((1,), (1,)), ((), ())), preferred_element_type=F32))
        row = core * TOK + t * 32 + lax.broadcasted_iota(jnp.int32, (32 * QH, 2 * TOK), 0) // QH
        col = lax.broadcasted_iota(jnp.int32, (32 * QH, 2 * TOK), 1)
        scores[chips] = jnp.where(col <= row, scores[chips], -1e30)
        top = functools.reduce(jnp.maximum, scores)
        top = jnp.max(top, axis=1, keepdims=True)
        total = None
        acc = None
        for b in range(chips + 1):
            p = jnp.exp2((scores[b] - top) * SCALE2)
            total = p if total is None else total + p
            v = lall[2 * b : 2 * b + 2, c, :, D : 2 * D].reshape(2 * TOK, D)
            part = jnp.dot(p.astype(BF16), v, preferred_element_type=F32)
            acc = part if acc is None else acc + part
        total = jnp.sum(total, axis=1, keepdims=True)
        otile[...] = acc * (1.0 / total)
        for e in range(QH):
            rows = otile[pl.ds(e, 32, stride=QH), :].astype(BF16)
            lout[c, pl.ds(pl.multiple_of(t * 32, 32), 32), e * D : (e + 1) * D] = rows

    for chips in range(4):
        @pl.when(x == chips)
        def _(chips=chips):
            @pl.loop(0, 32)
            def _(i):
                long_tile(i, chips)

    def out_copy(c):
        return pltpu.make_async_copy(
            lout.at[c], long_out.at[:, pl.ds(pl.multiple_of(c * QH * D, QH * D), QH * D)], loc_sem.at[8 + c])

    for c in range(NH):
        out_copy(c).start()

    l_pair.wait_send()
    for n in range(1, 4):
        @pl.when(x + n < 4)
        def _(n=n):
            l_copy(n).wait_send()

        @pl.when(x >= n)
        def _(n=n):
            f_copy(n).wait_send()

    @pl.loop(0, NG)
    def _(i):
        @pl.when(i != SELF)
        def _():
            _, source = group_at(i)
            pltpu.make_async_remote_copy(
                send.at[i], recv_out.at[source], z_send.at[i], z_recv.at[i],
                device_id=(source, h), device_id_type=MESH).wait()

    own_slot.wait()
    for c in range(NH):
        out_copy(c).wait()


def exchange(sq, skv, lq, lkv, tabs):
    any_spec = pl.BlockSpec(memory_space=pl.ANY)
    smem = pl.BlockSpec(memory_space=pltpu.SMEM)
    dma = pltpu.SemaphoreType.DMA
    return pl.pallas_call(
        main_kernel,
        out_shape=(
            jax.ShapeDtypeStruct((NG, SLOT, D), BF16),
            jax.ShapeDtypeStruct((TOK, NH * QH * D), BF16),
        ),
        in_specs=[any_spec] * 4 + [smem],
        out_specs=(any_spec, any_spec),
        scratch_shapes=[
            pltpu.VMEM((NH * TOK + DOC, QH, D), BF16),
            pltpu.VMEM(((NH * TOK + KROWS) // TB, TB, 2 * D), BF16),
            pltpu.VMEM((NG, SLOT, D), BF16),
            pltpu.VMEM((NH, NH, TOK, 2 * D), BF16),
            pltpu.VMEM((TOK, NH, QH, D), BF16),
            pltpu.VMEM((NH, TOK, QH * D), BF16),
            pltpu.VMEM((32 * QH, D), F32),
            dma((NH,)), dma((NH,)), dma((NH,)), dma((NH,)),
            dma((NG,)), dma((NG,)),
            dma((4,)), dma((4,)), dma((4,)), dma((4,)),
            dma((16,)),
        ],
        compiler_params=pltpu.CompilerParams(collective_id=0, has_side_effects=True),
        name="exchange",
    )(sq, skv, lq, lkv, tabs)


def place_kernel(per_step, got, long_in, short_out, long_out):
    long_out[...] = long_in[...]
    for s in range(per_step):
        v = got[s, WROWS:SLOT, :]
        for b in range(NB):
            w = got[s, wrow(b) : wrow(b + 1), :]
            o = lax.dot_general(w, v[: TB * (b + 1)], (((0,), (0,)), ((), ())), preferred_element_type=F32)
            o = o.astype(BF16)
            at = s * DOC + b * TB
            for e in range(QH):
                short_out[at : at + TB, e * D : (e + 1) * D] = o[e * TB : (e + 1) * TB, :]


def place(got, long_in):
    per_step = 4
    steps = NG // per_step
    return pl.pallas_call(
        functools.partial(place_kernel, per_step),
        grid=(steps,),
        out_shape=(
            jax.ShapeDtypeStruct((NG * DOC, QH * D), BF16),
            jax.ShapeDtypeStruct((TOK, NH * QH * D), BF16),
        ),
        in_specs=[
            pl.BlockSpec((per_step, SLOT, D), lambda i: (i, 0, 0)),
            pl.BlockSpec((TOK // steps, NH * QH * D), lambda i: (i, 0)),
        ],
        out_specs=(
            pl.BlockSpec((per_step * DOC, QH * D), lambda i: (i, 0)),
            pl.BlockSpec((TOK // steps, NH * QH * D), lambda i: (i, 0)),
        ),
        name="place",
    )(got, long_in)


def slot_tables(doc_lengths, destinations):
    g = lax.axis_index("grp")
    lens = lax.dynamic_index_in_dim(doc_lengths, g, 0, keepdims=False)
    dest = lax.dynamic_index_in_dim(destinations, g, 0, keepdims=False)
    doc = jnp.arange(NG, dtype=jnp.int32)
    hit = dest[None, :] == doc[:, None]
    before = jnp.where(doc[None, :] < doc[:, None], lens[None, :], 0).sum(axis=1)
    start = jnp.where(hit, before[None, :], 0).sum(axis=1)
    rows = jnp.where(hit, lens[None, :], 0).sum(axis=1)
    return jnp.stack([start, rows, start // TB, start % TB])


def on_device(long_queries, long_pairs, short_queries, short_pairs, doc_lengths, destinations):
    split = (TOK, NH, QH, D)
    got, long_mix = exchange(
        short_queries.reshape(split),
        jnp.transpose(short_pairs, (1, 0, 2)).reshape(NH, TOK // TB, TB, 2 * D),
        long_queries.reshape(split),
        jnp.transpose(long_pairs, (1, 0, 2)),
        slot_tables(doc_lengths, destinations),
    )
    short_placed, long_result = place(got, long_mix)
    return long_result, short_placed


def solution(mesh):
    rows = P(("grp", "head"), None, None)
    return jax.shard_map(
        on_device,
        mesh=mesh,
        in_specs=(rows, rows, rows, rows, P(), P()),
        out_specs=(P(("grp", "head"), None), P("grp", "head")),
        check_vma=False,
    )
```

time: 299 us -> 104 us (0.35); the launches traced: 294 us -> 104 us
  waiting for transfers between devices: 130 us -> 0 us
  Pallas kernels: 0 us -> 98 us
  local copies, waits for them, and re-layouts: 63.8 us -> 4.59 us
  starting transfers between devices: 45 us -> 0 us
  matrix products: 32.9 us -> 0 us
  other arithmetic: 21.3 us -> 0.82 us
    all_to_all x7 -> x0, waiting for transfers between devices: 130 us -> none  [the longest x1 90.8 us: on_device(): lax.all_to_all(slot_queries, 'grp', split_axis=0, concat_axis=0, tiled=True)]
    pallas_call x0 -> x2, Pallas kernels: none -> 98 us  [the longest x1 89.7 us: exchange(): pl.pallas_call(main_kernel, out_shape=(jax.ShapeDtypeStruct((NG, SLOT, D)...]
    all_to_all x7 -> x0, starting transfers between devices: 45 us -> none  [the longest x1 11.3 us: on_device(): lax.all_to_all(slot_pairs, 'grp', split_axis=0, concat_axis=0, tiled=True)]
    dot_general x6 -> x0, matrix products: 32.9 us -> none  [the longest x3 18.3 us: attend_rows(): jnp.einsum('qhgd,khd->hgqk', grouped, key_part, preferred_element_type=jn...]
    gather x3 -> x0, local copies, waits for them, and re-layouts: 28.9 us -> none  [the longest x2 19.9 us: on_device(): slot_queries = group_queries[row_index]]
    reduce_sum x5 -> x2, other arithmetic: 17.5 us -> 0.23 us  [the longest x1 0.11 us: slot_tables(): rows = jnp.where(hit, lens[None, :], 0).sum(axis=1)]
    unnamed x19 -> x1, local copies, waits for them, and re-layouts: 16.8 us -> 1.94 us
    transpose x1, local copies, waits for them, and re-layouts: 8.14 us -> 1.94 us  [on_device(): jnp.transpose(short_pairs, (1, 0, 2)).reshape(NH, TOK // TB, TB, 2 * D)]
  transfers between devices with their start and end apart: 7 -> 0, of which waited for: 6 -> 0; matrix products, arithmetic and copies ran while one was open for 31% -> 0% of each run, Pallas kernels for 0% -> 0%
where the time goes in v1:
time: 104 us
  Pallas kernels  98 us (94%)
  local copies, waits for them, and re-layouts  4.59 us (4%)
    pallas_call x1, Pallas kernels, exchange(): pl.pallas_call(main_kernel, out_shape=(jax.ShapeDtypeStruct((NG, SLOT, D)...  89.7 us
    pallas_call x1, Pallas kernels, place(): pl.pallas_call(functools.partial(place_kernel, per_step), grid=(steps,),...  8.28 us

profile of v1, /device:TPU:6, one launch (start us, length us, event | category | flops | bytes accessed | tf_op | source)
XLA Modules:
  0.0 104.1 jit_solution(17951140696043391129)
XLA Ops:
  0.6 0.7 dynamic-slice_bitcast_fusion
  1.3 0.1 select_reduce_fusion.2
  1.5 0.1 select_reduce_fusion
  1.6 0.6 pad_add_fusion.tabs
  2.2 1.9 %copy.13 = bf16[128,8,256]{2,0,1:T(8,128)(2,1)} copy(bf16[128,8,256]{2,1,0:T(8,128)(2,1)} %param.7) | data formatting | bytes 1048576 | tf_op args[1]
  4.1 1.9 %copy.10 = bf16[8,128,256]{2,1,0:T(8,128)(2,1)} copy(bf16[8,128,256]{2,0,1:T(8,128)(2,1)} %bitcast.23) | data formatting | bytes 1048576 | tf_op jit(solution)/shard_map/transpose | solution.py:349
  6.1 89.7 %exchange.1 = (bf16[32,224,128]{2,1,0:T(8,128)(2,1)}, bf16[128,8192]{1,0:T(8,128)(2,1)}) custom-call(bf16[128,8,8,128]{3,2,1,0:T(8,128)(2,1)} %bitcast.19, bf16[8,8,16,256]{3,2,1,0:T(8,128)(2,1)} %bitcast.22, bf16[128,8,8,128]{3,2,1,0:T(8,128)(2,1)} %bitcast.20, bf16[8,128,256]{2,1,0:T(8,128)(2,1)} %bitcast.21, s32[4,32]{1,0:T(4,128)} %pad_add_fusion.tabs), custom_call_target="tpu_custom_call" | custom-call | tf_op jit(solution)/shard_map/exchange/pallas_call | solution.py:272
  95.8 8.3 %place.1 = (bf16[2048,1024]{1,0:T(8,128)(2,1)}, bf16[128,8192]{1,0:T(8,128)(2,1)}) custom-call(bf16[32,224,128]{2,1,0:T(8,128)(2,1)} %get-tuple-element.6.got, bf16[128,8192]{1,0:T(8,128)(2,1)} %get-tuple-element.7.long_in), custom_call_target="tpu_custom_call" | custom-call | tf_op jit(solution)/shard_map/place/pallas_call | solution.py:314
  (1 shorter events, 0.0 us)

commit v2 on v1

v2 whole, which is shorter than its diff:
```python
import functools
import math

import jax
import jax.numpy as jnp
from jax import lax
from jax.experimental import pallas as pl
from jax.experimental.pallas import tpu as pltpu
from jax.sharding import PartitionSpec as P

MESH = pl.DeviceIdType.MESH
BF16 = jnp.bfloat16
F32 = jnp.float32

NG = 32
NH = 8
TOK = 128
QH = 8
D = 128
DOC = 64
TB = 16
NB = DOC // TB
WROWS = TB * NB * (NB + 1) // 2
SLOT = WROWS + DOC
KROWS = DOC + TB
SCALE2 = math.log2(math.e) / math.sqrt(D)


def wrow(block):
    return TB * block * (block + 1) // 2


def perm_matrix():
    row = lax.broadcasted_iota(jnp.int32, (D, D), 0)
    col = lax.broadcasted_iota(jnp.int32, (D, D), 1)
    return (col == (row % QH) * TB + row // QH).astype(BF16)


def slot_weights(q, k, length, perm):
    st = lax.dot_general(k, q, (((1,), (1,)), ((), ())), preferred_element_type=F32)
    out = []
    for b in range(NB):
        keys = TB * (b + 1)
        s = st[:keys, b * D : (b + 1) * D]
        key = lax.broadcasted_iota(jnp.int32, (keys, D), 0)
        tok = TB * b + lax.broadcasted_iota(jnp.int32, (keys, D), 1) // QH
        s = jnp.where(key <= tok, s, -1e30)
        top = jnp.max(s, axis=0, keepdims=True)
        p = jnp.exp2((s - top) * SCALE2)
        inv = 1.0 / jnp.sum(p, axis=0, keepdims=True)
        inv = jnp.where(tok[:1] < length, inv, 0.0)
        w = (p * inv).astype(BF16)
        w = jnp.dot(w, perm, preferred_element_type=F32).astype(BF16)
        out.append(w)
    return out


def main_kernel(
    sq, spair, lq, lpair, tabs,
    recv_out, long_out,
    gq, gkv, pbuf, skv, lkv, kscr, vscr, kslot, send, lall, lqv, lout, acc, mx, sm, otile,
    xq_send, xq_recv, xk_send, xk_recv, z_send, z_recv, v_send, v_recv,
    l_send, l_recv, f_send, f_recv, loc_sem,
):
    g = lax.axis_index("grp")
    h = lax.axis_index("head")
    y, z = g // 8, g % 8
    x, core = h // 2, h % 2

    def group_at(i):
        m = i % 8
        oz = jnp.where(m % 2 == 0, m // 2 + 1, 8 - (m // 2 + 1))
        oz = jnp.where(m == 7, 0, oz)
        oy = i // 8
        return ((y + oy) % 4) * 8 + (z + oz) % 8, ((y + 4 - oy) % 4) * 8 + (z + 8 - oz) % 8

    SELF = 7

    barrier = pltpu.get_barrier_semaphore()

    @pl.loop(1, NG)
    def _(o):
        pl.semaphore_signal(barrier, inc=1, device_id=((g + o) % NG, h), device_id_type=MESH)

    for o in range(1, NH):
        pl.semaphore_signal(barrier, inc=1, device_id=(g, (h + o) % NH), device_id_type=MESH)

    own = pl.ds(pl.multiple_of(h * TOK, TOK), TOK)
    own_kv = pl.ds(h * (TOK // TB), TOK // TB)
    in_sp = pltpu.make_async_copy(spair, pbuf.at[0], loc_sem.at[0])
    in_lp = pltpu.make_async_copy(lpair, pbuf.at[1], loc_sem.at[1])
    in_lq = pltpu.make_async_copy(lq, lqv, loc_sem.at[2])
    own_q = pltpu.make_async_copy(sq.at[:, h], gq.at[own], loc_sem.at[3])
    in_sp.start()
    in_lp.start()
    in_lq.start()
    own_q.start()

    def by_head(n, store):
        for t in range(TOK // 32):
            part = pbuf[n, t * 32 : (t + 1) * 32].astype(F32).reshape(32 * NH, 2 * D)
            kscr[t * 32 * NH : (t + 1) * 32 * NH, :] = part[:, :D]
            vscr[t * 32 * NH : (t + 1) * 32 * NH, :] = part[:, D:]
        for c in range(NH):
            store(c, kscr[pl.ds(c, TOK, stride=NH), :].astype(BF16), vscr[pl.ds(c, TOK, stride=NH), :].astype(BF16))

    def store_short(c, k, v):
        skv[c, :, :, :D] = k.reshape(TOK // TB, TB, D)
        skv[c, :, :, D:] = v.reshape(TOK // TB, TB, D)

    def store_long(c, k, v):
        lkv[c, :, :D] = k
        lkv[c, :, D:] = v

    in_sp.wait()
    by_head(0, store_short)
    gq[NH * TOK :, :, :] = jnp.zeros((DOC, QH, D), BF16)
    gkv[NH * TOK // TB :] = jnp.zeros((KROWS // TB, TB, 2 * D), BF16)
    pl.semaphore_wait(barrier, NH - 1 + NG - 1)

    def k_copy(o):
        peer = (h + o) % NH
        return pltpu.make_async_remote_copy(
            skv.at[peer], gkv.at[own_kv], xk_send.at[o], xk_recv.at[o],
            device_id=(g, peer), device_id_type=MESH)

    def q_copy(o):
        peer = (h + o) % NH
        return pltpu.make_async_remote_copy(
            sq.at[:, peer], gq.at[own], xq_send.at[o], xq_recv.at[o],
            device_id=(g, peer), device_id_type=MESH)

    for o in range(1, NH):
        k_copy(o).start()
    for o in range(1, NH):
        q_copy(o).start()
    own_k = pltpu.make_async_copy(skv.at[h], gkv.at[own_kv], loc_sem.at[4])
    own_k.start()

    partner = h + 1 - 2 * core

    def l_copy(n):
        return pltpu.make_async_remote_copy(
            lkv, lall.at[h], l_send.at[n], l_recv.at[n],
            device_id=(g, (h + 2 * n) % NH), device_id_type=MESH)

    def f_copy(n):
        src = (h + NH - 2 * n) % NH
        return pltpu.make_async_remote_copy(
            lall.at[src], lall.at[src], f_send.at[n], f_recv.at[n],
            device_id=(g, partner), device_id_type=MESH)

    l_pair = pltpu.make_async_remote_copy(
        lkv, lall.at[h], f_send.at[0], f_recv.at[0],
        device_id=(g, partner), device_id_type=MESH)
    own_l = pltpu.make_async_copy(lkv, lall.at[h], loc_sem.at[5])

    in_lp.wait()
    by_head(1, store_long)
    l_pair.start()
    own_l.start()

    def v_copy(i):
        to, _ = group_at(i)
        return pltpu.make_async_remote_copy(
            send.at[i, pl.ds(WROWS, DOC)], recv_out.at[g, pl.ds(WROWS, DOC)], v_send.at[i], v_recv.at[i],
            device_id=(to, h), device_id_type=MESH)

    def z_copy(i):
        to, _ = group_at(i)
        return pltpu.make_async_remote_copy(
            send.at[i, pl.ds(0, WROWS)], recv_out.at[g, pl.ds(0, WROWS)], z_send.at[i], z_recv.at[i],
            device_id=(to, h), device_id_type=MESH)

    def slot_pair(i):
        to, _ = group_at(i)
        kv = gkv[pl.ds(tabs[2, to], KROWS // TB)].reshape(KROWS, 2 * D)
        pick = lax.broadcasted_iota(jnp.int32, (DOC, KROWS), 0) + tabs[3, to]
        pick = (pick == lax.broadcasted_iota(jnp.int32, (DOC, KROWS), 1)).astype(BF16)
        kv = jnp.dot(pick, kv, preferred_element_type=F32).astype(BF16)
        kslot[i] = kv[:, :D]
        send[i, WROWS:SLOT, :] = kv[:, D:]

    perm = perm_matrix()

    def slot(i):
        to, _ = group_at(i)
        q = gq[pl.ds(tabs[0, to], DOC)].astype(F32).reshape(DOC * QH, D).astype(BF16)
        for b, w in enumerate(slot_weights(q, kslot[i], tabs[1, to], perm)):
            send[i, wrow(b) : wrow(b + 1), :] = w

    own_slot = pltpu.make_async_copy(send.at[SELF], recv_out.at[g], loc_sem.at[6])

    GROUP = 4

    def in_groups(work, copy):
        def start(j):
            for d in range(GROUP):
                i = j * GROUP + d

                @pl.when(i != SELF)
                def _(i=i):
                    copy(i).start()

        def step(j):
            for d in range(GROUP):
                work(j * GROUP + d)

        step(0)

        @pl.loop(1, NG // GROUP)
        def _(j):
            step(j)
            start(j - 1)

        start(jnp.int32(NG // GROUP - 1))

    own_k.wait()
    for o in range(1, NH):
        k_copy(o).wait_recv()
    in_groups(slot_pair, v_copy)

    R = 32
    M = R * QH
    TILES = NH * TOK // R

    def long_block(n, first):
        at = 2 * (x - n)

        def tile(i, _):
            c, t = i // (TOK // R), i % (TOK // R)
            rows = pl.ds(pl.multiple_of(i * M, M), M)
            q = lqv[pl.ds(t * R, R), c].astype(F32).reshape(M, D).astype(BF16)
            k = lall[pl.ds(at, 2), c, :, 0:D].reshape(2 * TOK, D)
            v = lall[pl.ds(at, 2), c, :, D : 2 * D].reshape(2 * TOK, D)
            s = lax.dot_general(q, k, (((1,), (1,)), ((), ())), preferred_element_type=F32)
            if first:
                row = core * TOK + t * R + lax.broadcasted_iota(jnp.int32, (M, 2 * TOK), 0) // QH
                col = lax.broadcasted_iota(jnp.int32, (M, 2 * TOK), 1)
                s = jnp.where(col <= row, s, -1e30)
            top = jnp.max(jnp.maximum(s[:, :D], s[:, D:]), axis=1, keepdims=True)
            top = jnp.broadcast_to(top, (M, D))
            if not first:
                old = mx[rows, :]
                top = jnp.maximum(old, top)
                fade = jnp.exp2((old - top) * SCALE2)
            p0 = jnp.exp2((s[:, :D] - top) * SCALE2)
            p1 = jnp.exp2((s[:, D:] - top) * SCALE2)
            p = jnp.concatenate([p0.astype(BF16), p1.astype(BF16)], axis=1)
            part = jnp.dot(p, v, preferred_element_type=F32)
            mx[rows, :] = top
            if first:
                sm[rows, :] = p0 + p1
                acc[rows, :] = part
            else:
                sm[rows, :] = sm[rows, :] * fade + (p0 + p1)
                acc[rows, :] = acc[rows, :] * fade + part
            return 0

        lax.fori_loop(0, TILES, tile, 0, unroll=8)

    in_lq.wait()
    own_l.wait()
    l_pair.wait_recv()
    long_block(0, True)

    own_q.wait()
    for o in range(1, NH):
        q_copy(o).wait_recv()
    for o in range(1, NH):
        k_copy(o).wait_send()
        q_copy(o).wait_send()
    for n in range(1, 4):
        @pl.when(x + n < 4)
        def _(n=n):
            l_copy(n).start()

    in_groups(slot, z_copy)
    own_slot.start()

    for n in range(1, 4):
        @pl.when(x >= n)
        def _(n=n):
            l_copy(n).wait_recv()
            f_copy(n).start()

    @pl.loop(1, x + 1)
    def _(n):
        f_copy(n).wait_recv()
        long_block(n, False)

    def out_copy(c):
        return pltpu.make_async_copy(
            lout.at[c], long_out.at[:, pl.ds(pl.multiple_of(c * QH * D, QH * D), QH * D)], loc_sem.at[8 + c])

    @pl.loop(0, NH)
    def _(c):
        for t in range(TOK // R):
            rows = pl.ds(pl.multiple_of((c * (TOK // R) + t) * M, M), M)
            total = jnp.sum(sm[rows, :], axis=1, keepdims=True)
            otile[t * M : (t + 1) * M, :] = acc[rows, :] * (1.0 / total)
        for t in range(TOK // R):
            for e in range(QH):
                part = otile[pl.ds(t * M + e, R, stride=QH), :].astype(BF16)
                lout[c, t * R : (t + 1) * R, e * D : (e + 1) * D] = part
        out_copy(c).start()

    l_pair.wait_send()
    for n in range(1, 4):
        @pl.when(x + n < 4)
        def _(n=n):
            l_copy(n).wait_send()

        @pl.when(x >= n)
        def _(n=n):
            f_copy(n).wait_send()

    @pl.loop(0, NG)
    def _(i):
        @pl.when(i != SELF)
        def _():
            _, source = group_at(i)
            for lo, size, ss, rs in ((WROWS, DOC, v_send, v_recv), (0, WROWS, z_send, z_recv)):
                pltpu.make_async_remote_copy(
                    send.at[i, pl.ds(lo, size)], recv_out.at[source, pl.ds(lo, size)], ss.at[i], rs.at[i],
                    device_id=(source, h), device_id_type=MESH).wait()

    own_slot.wait()
    for c in range(NH):
        out_copy(c).wait()


def exchange(sq, spair, lq, lpair, tabs):
    any_spec = pl.BlockSpec(memory_space=pl.ANY)
    smem = pl.BlockSpec(memory_space=pltpu.SMEM)
    dma = pltpu.SemaphoreType.DMA
    return pl.pallas_call(
        main_kernel,
        out_shape=(
            jax.ShapeDtypeStruct((NG, SLOT, D), BF16),
            jax.ShapeDtypeStruct((TOK, NH * QH * D), BF16),
        ),
        in_specs=[any_spec] * 4 + [smem],
        out_specs=(any_spec, any_spec),
        scratch_shapes=[
            pltpu.VMEM((NH * TOK + DOC, QH, D), BF16),
            pltpu.VMEM(((NH * TOK + KROWS) // TB, TB, 2 * D), BF16),
            pltpu.VMEM((2, TOK, NH, 2 * D), BF16),
            pltpu.VMEM((NH, TOK // TB, TB, 2 * D), BF16),
            pltpu.VMEM((NH, TOK, 2 * D), BF16),
            pltpu.VMEM((TOK * NH, D), F32),
            pltpu.VMEM((TOK * NH, D), F32),
            pltpu.VMEM((NG, DOC, D), BF16),
            pltpu.VMEM((NG, SLOT, D), BF16),
            pltpu.VMEM((NH, NH, TOK, 2 * D), BF16),
            pltpu.VMEM((TOK, NH, QH, D), BF16),
            pltpu.VMEM((NH, TOK, QH * D), BF16),
            pltpu.VMEM((TOK * NH * QH, D), F32),
            pltpu.VMEM((TOK * NH * QH, D), F32),
            pltpu.VMEM((TOK * NH * QH, D), F32),
            pltpu.VMEM((TOK * QH, D), F32),
            dma((NH,)), dma((NH,)), dma((NH,)), dma((NH,)),
            dma((NG,)), dma((NG,)), dma((NG,)), dma((NG,)),
            dma((4,)), dma((4,)), dma((4,)), dma((4,)),
            dma((16,)),
        ],
        compiler_params=pltpu.CompilerParams(collective_id=0, has_side_effects=True),
        name="exchange",
    )(sq, spair, lq, lpair, tabs)


def place_kernel(per_step, got, long_in, short_out, long_out):
    long_out[...] = long_in[...]
    for s in range(per_step):
        v = got[s, WROWS:SLOT, :]
        for b in range(NB):
            w = got[s, wrow(b) : wrow(b + 1), :]
            o = lax.dot_general(w, v[: TB * (b + 1)], (((0,), (0,)), ((), ())), preferred_element_type=F32)
            o = o.astype(BF16)
            at = s * DOC + b * TB
            for e in range(QH):
                short_out[at : at + TB, e * D : (e + 1) * D] = o[e * TB : (e + 1) * TB, :]


def place(got, long_in):
    per_step = 4
    steps = NG // per_step
    return pl.pallas_call(
        functools.partial(place_kernel, per_step),
        grid=(steps,),
        out_shape=(
            jax.ShapeDtypeStruct((NG * DOC, QH * D), BF16),
            jax.ShapeDtypeStruct((TOK, NH * QH * D), BF16),
        ),
        in_specs=[
            pl.BlockSpec((per_step, SLOT, D), lambda i: (i, 0, 0)),
            pl.BlockSpec((TOK // steps, NH * QH * D), lambda i: (i, 0)),
        ],
        out_specs=(
            pl.BlockSpec((per_step * DOC, QH * D), lambda i: (i, 0)),
            pl.BlockSpec((TOK // steps, NH * QH * D), lambda i: (i, 0)),
        ),
        name="place",
    )(got, long_in)


def slot_tables(doc_lengths, destinations):
    g = lax.axis_index("grp")
    lens = lax.dynamic_index_in_dim(doc_lengths, g, 0, keepdims=False)
    dest = lax.dynamic_index_in_dim(destinations, g, 0, keepdims=False)
    doc = jnp.arange(NG, dtype=jnp.int32)
    hit = dest[None, :] == doc[:, None]
    before = jnp.where(doc[None, :] < doc[:, None], lens[None, :], 0).sum(axis=1)
    start = jnp.where(hit, before[None, :], 0).sum(axis=1)
    rows = jnp.where(hit, lens[None, :], 0).sum(axis=1)
    return jnp.stack([start, rows, start // TB, start % TB])


def on_device(long_queries, long_pairs, short_queries, short_pairs, doc_lengths, destinations):
    split = (TOK, NH, QH, D)
    got, long_mix = exchange(
        short_queries.reshape(split),
        short_pairs,
        long_queries.reshape(split),
        long_pairs,
        slot_tables(doc_lengths, destinations),
    )
    short_placed, long_result = place(got, long_mix)
    return long_result, short_placed


def solution(mesh):
    rows = P(("grp", "head"), None, None)
    return jax.shard_map(
        on_device,
        mesh=mesh,
        in_specs=(rows, rows, rows, rows, P(), P()),
        out_specs=(P(("grp", "head"), None), P("grp", "head")),
        check_vma=False,
    )
```

time: 104 us -> 94 us (0.904); the launches traced: 104 us -> 92.2 us
  Pallas kernels: 98 us -> 90 us
  local copies, waits for them, and re-layouts: 4.59 us -> 0.71 us
    pallas_call x1, Pallas kernels: 89.7 us -> 81.7 us  [exchange(): pl.pallas_call(main_kernel, out_shape=(jax.ShapeDtypeStruct((NG, SLOT, D)...]
    transpose x1 -> x0, local copies, waits for them, and re-layouts: 1.94 us -> none  [on_device(): jnp.transpose(short_pairs, (1, 0, 2)).reshape(NH, TOK // TB, TB, 2 * D)]
    unnamed x1 -> x0, local copies, waits for them, and re-layouts: 1.94 us -> none
where the time goes in v2:
time: 94 us; the launch traced here: 92.2 us
  Pallas kernels  90 us (96%)
    pallas_call x1, Pallas kernels, exchange(): pl.pallas_call(main_kernel, out_shape=(jax.ShapeDtypeStruct((NG, SLOT, D)...  81.7 us
    pallas_call x1, Pallas kernels, place(): pl.pallas_call(functools.partial(place_kernel, per_step), grid=(steps,),...  8.29 us

profile of v2, /device:TPU:6, one launch (start us, length us, event | category | flops | bytes accessed | tf_op | source)
XLA Modules:
  0.0 92.2 jit_solution(14425931052165042465)
XLA Ops:
  0.6 0.7 dynamic-slice_bitcast_fusion
  1.3 0.1 select_reduce_fusion.2
  1.5 0.1 select_reduce_fusion
  1.6 0.6 pad_add_fusion.tabs
  2.2 81.7 %exchange.1 = (bf16[32,224,128]{2,1,0:T(8,128)(2,1)}, bf16[128,8192]{1,0:T(8,128)(2,1)}) custom-call(bf16[128,8,8,128]{3,2,1,0:T(8,128)(2,1)} %bitcast.14, bf16[128,8,256]{2,1,0:T(8,128)(2,1)} %spair.1, bf16[128,8,8,128]{3,2,1,0:T(8,128)(2,1)} %bitcast.15, bf16[128,8,256]{2,1,0:T(8,128)(2,1)} %lpair.1, s32[4,32]{1,0:T(4,128)} %pad_add_fusion.tabs), custom_call_target="tpu_custom_call" | custom-call | tf_op jit(solution)/shard_map/exchange/pallas_call | solution.py:337
  83.9 8.3 %place.1 = (bf16[2048,1024]{1,0:T(8,128)(2,1)}, bf16[128,8192]{1,0:T(8,128)(2,1)}) custom-call(bf16[32,224,128]{2,1,0:T(8,128)(2,1)} %get-tuple-element.6.got, bf16[128,8192]{1,0:T(8,128)(2,1)} %get-tuple-element.7.long_in), custom_call_target="tpu_custom_call" | custom-call | tf_op jit(solution)/shard_map/place/pallas_call | solution.py:388
  (1 shorter events, 0.0 us)

commit v3 on v2

--- a/solution.py
+++ b/solution.py
@@ -98,7 +98,7 @@
 
     def by_head(n, store):
         for t in range(TOK // 32):
-            part = pbuf[n, t * 32 : (t + 1) * 32].astype(F32).reshape(32 * NH, 2 * D)
+            part = pbuf[n, t].astype(F32).reshape(32 * NH, 2 * D)
             kscr[t * 32 * NH : (t + 1) * 32 * NH, :] = part[:, :D]
             vscr[t * 32 * NH : (t + 1) * 32 * NH, :] = part[:, D:]
         for c in range(NH):
@@ -278,14 +278,10 @@
     in_groups(slot, z_copy)
     own_slot.start()
 
-    for n in range(1, 4):
-        @pl.when(x >= n)
-        def _(n=n):
-            l_copy(n).wait_recv()
-            f_copy(n).start()
-
     @pl.loop(1, x + 1)
     def _(n):
+        l_copy(n).wait_recv()
+        f_copy(n).start()
         f_copy(n).wait_recv()
         long_block(n, False)
 
@@ -345,7 +341,7 @@
         scratch_shapes=[
             pltpu.VMEM((NH * TOK + DOC, QH, D), BF16),
             pltpu.VMEM(((NH * TOK + KROWS) // TB, TB, 2 * D), BF16),
-            pltpu.VMEM((2, TOK, NH, 2 * D), BF16),
+            pltpu.VMEM((2, TOK // 32, 32, NH, 2 * D), BF16),
             pltpu.VMEM((NH, TOK // TB, TB, 2 * D), BF16),
             pltpu.VMEM((NH, TOK, 2 * D), BF16),
             pltpu.VMEM((TOK * NH, D), F32),
@@ -364,42 +360,72 @@
             dma((4,)), dma((4,)), dma((4,)), dma((4,)),
             dma((16,)),
         ],
-        compiler_params=pltpu.CompilerParams(collective_id=0, has_side_effects=True),
+        compiler_params=pltpu.CompilerParams(
+            collective_id=0, has_side_effects=True, vmem_limit_bytes=48 << 20),
         name="exchange",
     )(sq, spair, lq, lpair, tabs)
 
 
-def place_kernel(per_step, got, long_in, short_out, long_out):
-    long_out[...] = long_in[...]
-    for s in range(per_step):
-        v = got[s, WROWS:SLOT, :]
-        for b in range(NB):
-            w = got[s, wrow(b) : wrow(b + 1), :]
-            o = lax.dot_general(w, v[: TB * (b + 1)], (((0,), (0,)), ((), ())), preferred_element_type=F32)
-            o = o.astype(BF16)
-            at = s * DOC + b * TB
-            for e in range(QH):
-                short_out[at : at + TB, e * D : (e + 1) * D] = o[e * TB : (e + 1) * TB, :]
-
-
-def place(got, long_in):
+def place_kernel(got, long_in, short_out, long_out, gbuf, obuf, lbuf, in_sem, out_sem, l_sem):
     per_step = 4
     steps = NG // per_step
+
+    def g_copy(j):
+        part = pl.ds(j * per_step, per_step)
+        return pltpu.make_async_copy(got.at[part], gbuf.at[part], in_sem.at[j])
+
+    def o_copy(j):
+        part = pl.ds(pl.multiple_of(j * per_step * DOC, per_step * DOC), per_step * DOC)
+        return pltpu.make_async_copy(obuf.at[part], short_out.at[part], out_sem.at[j])
+
+    l_get = pltpu.make_async_copy(long_in, lbuf, l_sem.at[0])
+    l_put = pltpu.make_async_copy(lbuf, long_out, l_sem.at[1])
+    for j in range(steps):
+        g_copy(j).start()
+    l_get.start()
+
+    def step(j, _):
+        g_copy(j).wait()
+        for d in range(per_step):
+            s = j * per_step + d
+            v = gbuf[s, WROWS:SLOT, :]
+            for b in range(NB):
+                w = gbuf[s, wrow(b) : wrow(b + 1), :]
+                o = lax.dot_general(w, v[: TB * (b + 1)], (((0,), (0,)), ((), ())), preferred_element_type=F32)
+                o = o.astype(BF16)
+                rows = pl.ds(pl.multiple_of(s * DOC + b * TB, TB), TB)
+                for e in range(QH):
+                    obuf[rows, e * D : (e + 1) * D] = o[e * TB : (e + 1) * TB, :]
+        o_copy(j).start()
+        return 0
+
+    step(0, 0)
+    l_get.wait()
+    l_put.start()
+    lax.fori_loop(1, steps, step, 0)
+    for j in range(steps):
+        o_copy(j).wait()
+    l_put.wait()
+
+
+def place(got, long_in):
+    any_spec = pl.BlockSpec(memory_space=pl.ANY)
+    dma = pltpu.SemaphoreType.DMA
     return pl.pallas_call(
-        functools.partial(place_kernel, per_step),
-        grid=(steps,),
+        place_kernel,
         out_shape=(
             jax.ShapeDtypeStruct((NG * DOC, QH * D), BF16),
             jax.ShapeDtypeStruct((TOK, NH * QH * D), BF16),
         ),
-        in_specs=[
-            pl.BlockSpec((per_step, SLOT, D), lambda i: (i, 0, 0)),
-            pl.BlockSpec((TOK // steps, NH * QH * D), lambda i: (i, 0)),
+        in_specs=[any_spec, any_spec],
+        out_specs=(any_spec, any_spec),
+        scratch_shapes=[
+            pltpu.VMEM((NG, SLOT, D), BF16),
+            pltpu.VMEM((NG * DOC, QH * D), BF16),
+            pltpu.VMEM((TOK, NH * QH * D), BF16),
+            dma((8,)), dma((8,)), dma((2,)),
         ],
-        out_specs=(
-            pl.BlockSpec((per_step * DOC, QH * D), lambda i: (i, 0)),
-            pl.BlockSpec((TOK // steps, NH * QH * D), lambda i: (i, 0)),
-        ),
+        compiler_params=pltpu.CompilerParams(vmem_limit_bytes=24 << 20),
         name="place",
     )(got, long_in)
 
@@ -417,12 +443,17 @@
 
 
 def on_device(long_queries, long_pairs, short_queries, short_pairs, doc_lengths, destinations):
-    split = (TOK, NH, QH, D)
+    queries = (TOK, NH, QH, D)
+    pairs = (TOK // 32, 32, NH, 2 * D)
+
+    def stay(array, shape):
+        return pltpu.with_memory_space_constraint(array.reshape(shape), pltpu.HBM)
+
     got, long_mix = exchange(
-        short_queries.reshape(split),
-        short_pairs,
-        long_queries.reshape(split),
-        long_pairs,
+        stay(short_queries, queries),
+        stay(short_pairs, pairs),
+        stay(long_queries, queries),
+        stay(long_pairs, pairs),
         slot_tables(doc_lengths, destinations),
     )
     short_placed, long_result = place(got, long_mix)

time: 94 us -> 84.5 us (0.90); the launches traced: 92.2 us -> 84.3 us
  Pallas kernels: 90 us -> 82.7 us
    pallas_call x1, Pallas kernels: 81.7 us -> 76.5 us  [exchange(): pl.pallas_call(main_kernel, out_shape=(jax.ShapeDtypeStruct((NG, SLOT, D)...]
    pallas_call x1, Pallas kernels: 8.29 us -> 6.15 us  [place(): pl.pallas_call(place_kernel, out_shape=(jax.ShapeDtypeStruct((NG * DOC, Q...]
where the time goes in v3:
time: 84.5 us; the launch traced here: 84.3 us
  Pallas kernels  82.7 us (98%)
    pallas_call x1, Pallas kernels, exchange(): pl.pallas_call(main_kernel, out_shape=(jax.ShapeDtypeStruct((NG, SLOT, D)...  76.5 us
    pallas_call x1, Pallas kernels, place(): pl.pallas_call(place_kernel, out_shape=(jax.ShapeDtypeStruct((NG * DOC, Q...  6.15 us

profile of v3, /device:TPU:6, one launch (start us, length us, event | category | flops | bytes accessed | tf_op | source)
XLA Modules:
  0.0 84.3 jit_solution(6766638267382003102)
XLA Ops:
  0.6 0.7 dynamic-slice_bitcast_fusion
  1.3 0.1 select_reduce_fusion.2
  1.5 0.1 select_reduce_fusion
  1.6 76.5 %exchange.1 = (bf16[32,224,128]{2,1,0:T(8,128)(2,1)S(1)}, bf16[128,8192]{1,0:T(8,128)(2,1)S(1)}) custom-call(bf16[128,8,8,128]{3,2,1,0:T(8,128)(2,1)} %bitcast.16, bf16[4,32,8,256]{3,2,1,0:T(8,128)(2,1)} %bitcast.18, bf16[128,8,8,128]{3,2,1,0:T(8,128)(2,1)} %bitcast.17, bf16[4,32,8,256]{3,2,1,0:T(8,128)(2,1)} %bitcast.19, s32[4,32]{1,0:T(4,128)S(1)} %pad_add_fusion.tabs), custom_call_target="tpu_custom_call" | custom-call | tf_op jit(solution)/shard_map/exchange/pallas_call | solution.py:333
  78.1 6.2 %place.1 = (bf16[2048,1024]{1,0:T(8,128)(2,1)}, bf16[128,8192]{1,0:T(8,128)(2,1)}) custom-call(bf16[32,224,128]{2,1,0:T(8,128)(2,1)S(1)} %get-tuple-element.6.got, bf16[128,8192]{1,0:T(8,128)(2,1)S(1)} %get-tuple-element.7.long_in), custom_call_target="tpu_custom_call" | custom-call | tf_op jit(solution)/shard_map/place/pallas_call | solution.py:414
  (2 shorter events, 0.0 us)

commit v4 on v3

--- a/solution.py
+++ b/solution.py
@@ -366,31 +366,22 @@
     )(sq, spair, lq, lpair, tabs)
 
 
-def place_kernel(got, long_in, short_out, long_out, gbuf, obuf, lbuf, in_sem, out_sem, l_sem):
+def place_kernel(got, long_in, short_out, long_out, obuf, out_sem, l_sem):
     per_step = 4
     steps = NG // per_step
-
-    def g_copy(j):
-        part = pl.ds(j * per_step, per_step)
-        return pltpu.make_async_copy(got.at[part], gbuf.at[part], in_sem.at[j])
 
     def o_copy(j):
         part = pl.ds(pl.multiple_of(j * per_step * DOC, per_step * DOC), per_step * DOC)
         return pltpu.make_async_copy(obuf.at[part], short_out.at[part], out_sem.at[j])
 
-    l_get = pltpu.make_async_copy(long_in, lbuf, l_sem.at[0])
-    l_put = pltpu.make_async_copy(lbuf, long_out, l_sem.at[1])
-    for j in range(steps):
-        g_copy(j).start()
-    l_get.start()
+    l_put = pltpu.make_async_copy(long_in, long_out, l_sem)
 
     def step(j, _):
-        g_copy(j).wait()
         for d in range(per_step):
             s = j * per_step + d
-            v = gbuf[s, WROWS:SLOT, :]
+            v = got[s, WROWS:SLOT, :]
             for b in range(NB):
-                w = gbuf[s, wrow(b) : wrow(b + 1), :]
+                w = got[s, wrow(b) : wrow(b + 1), :]
                 o = lax.dot_general(w, v[: TB * (b + 1)], (((0,), (0,)), ((), ())), preferred_element_type=F32)
                 o = o.astype(BF16)
                 rows = pl.ds(pl.multiple_of(s * DOC + b * TB, TB), TB)
@@ -399,10 +390,8 @@
         o_copy(j).start()
         return 0
 
-    step(0, 0)
-    l_get.wait()
     l_put.start()
-    lax.fori_loop(1, steps, step, 0)
+    lax.fori_loop(0, steps, step, 0)
     for j in range(steps):
         o_copy(j).wait()
     l_put.wait()
@@ -417,13 +406,11 @@
             jax.ShapeDtypeStruct((NG * DOC, QH * D), BF16),
             jax.ShapeDtypeStruct((TOK, NH * QH * D), BF16),
         ),
-        in_specs=[any_spec, any_spec],
+        in_specs=[pl.BlockSpec(memory_space=pltpu.VMEM), any_spec],
         out_specs=(any_spec, any_spec),
         scratch_shapes=[
-            pltpu.VMEM((NG, SLOT, D), BF16),
             pltpu.VMEM((NG * DOC, QH * D), BF16),
-            pltpu.VMEM((TOK, NH * QH * D), BF16),
-            dma((8,)), dma((8,)), dma((2,)),
+            dma((8,)), dma,
         ],
         compiler_params=pltpu.CompilerParams(vmem_limit_bytes=24 << 20),
         name="place",

time: 84.5 us -> 81.9 us (0.969)
  Pallas kernels: 82.7 us -> 80.1 us
    pallas_call x1, Pallas kernels: 6.15 us -> 3.57 us  [place(): pl.pallas_call(place_kernel, out_shape=(jax.ShapeDtypeStruct((NG * DOC, Q...]
where the time goes in v4:
time: 81.9 us; the launch traced here: 81.7 us
  Pallas kernels  80.1 us (98%)
    pallas_call x1, Pallas kernels, exchange(): pl.pallas_call(main_kernel, out_shape=(jax.ShapeDtypeStruct((NG, SLOT, D)...  76.5 us
    pallas_call x1, Pallas kernels, place(): pl.pallas_call(place_kernel, out_shape=(jax.ShapeDtypeStruct((NG * DOC, Q...  3.57 us

profile of v4, /device:TPU:6, one launch (start us, length us, event | category | flops | bytes accessed | tf_op | source)
XLA Modules:
  0.0 81.7 jit_solution(14543941990093526708)
XLA Ops:
  0.6 0.7 dynamic-slice_bitcast_fusion
  1.3 0.1 select_reduce_fusion.2
  1.5 0.1 select_reduce_fusion
  1.6 76.5 %exchange.1 = (bf16[32,224,128]{2,1,0:T(8,128)(2,1)S(1)}, bf16[128,8192]{1,0:T(8,128)(2,1)S(1)}) custom-call(bf16[128,8,8,128]{3,2,1,0:T(8,128)(2,1)} %bitcast.16, bf16[4,32,8,256]{3,2,1,0:T(8,128)(2,1)} %bitcast.18, bf16[128,8,8,128]{3,2,1,0:T(8,128)(2,1)} %bitcast.17, bf16[4,32,8,256]{3,2,1,0:T(8,128)(2,1)} %bitcast.19, s32[4,32]{1,0:T(4,128)S(1)} %pad_add_fusion.tabs), custom_call_target="tpu_custom_call" | custom-call | tf_op jit(solution)/shard_map/exchange/pallas_call | solution.py:333
  78.1 3.6 %place.1 = (bf16[2048,1024]{1,0:T(8,128)(2,1)}, bf16[128,8192]{1,0:T(8,128)(2,1)}) custom-call(bf16[32,224,128]{2,1,0:T(8,128)(2,1)S(1)} %get-tuple-element.6.got, bf16[128,8192]{1,0:T(8,128)(2,1)S(1)} %get-tuple-element.7.long_in), custom_call_target="tpu_custom_call" | custom-call | tf_op jit(solution)/shard_map/place/pallas_call | solution.py:403
  (2 shorter events, 0.0 us)

commit v5 on v4

--- a/solution.py
+++ b/solution.py
@@ -267,9 +267,6 @@
     own_q.wait()
     for o in range(1, NH):
         q_copy(o).wait_recv()
-    for o in range(1, NH):
-        k_copy(o).wait_send()
-        q_copy(o).wait_send()
     for n in range(1, 4):
         @pl.when(x + n < 4)
         def _(n=n):
@@ -301,6 +298,9 @@
                 lout[c, t * R : (t + 1) * R, e * D : (e + 1) * D] = part
         out_copy(c).start()
 
+    for o in range(1, NH):
+        k_copy(o).wait_send()
+        q_copy(o).wait_send()
     l_pair.wait_send()
     for n in range(1, 4):
         @pl.when(x + n < 4)

time: 81.9 us -> 80.7 us (0.985)
  Pallas kernels: 80.1 us -> 78.9 us
    pallas_call x1, Pallas kernels: 76.5 us -> 75.3 us  [exchange(): pl.pallas_call(main_kernel, out_shape=(jax.ShapeDtypeStruct((NG, SLOT, D)...]
where the time goes in v5:
time: 80.7 us; the launch traced here: 80.5 us
  Pallas kernels  78.9 us (98%)
    pallas_call x1, Pallas kernels, exchange(): pl.pallas_call(main_kernel, out_shape=(jax.ShapeDtypeStruct((NG, SLOT, D)...  75.3 us
    pallas_call x1, Pallas kernels, place(): pl.pallas_call(place_kernel, out_shape=(jax.ShapeDtypeStruct((NG * DOC, Q...  3.57 us

profile of v5, /device:TPU:6, one launch (start us, length us, event | category | flops | bytes accessed | tf_op | source)
XLA Modules:
  0.0 80.5 jit_solution(10019976915398671233)
XLA Ops:
  0.6 0.7 dynamic-slice_bitcast_fusion
  1.3 0.1 select_reduce_fusion.2
  1.5 0.1 select_reduce_fusion
  1.6 75.3 %exchange.1 = (bf16[32,224,128]{2,1,0:T(8,128)(2,1)S(1)}, bf16[128,8192]{1,0:T(8,128)(2,1)S(1)}) custom-call(bf16[128,8,8,128]{3,2,1,0:T(8,128)(2,1)} %bitcast.16, bf16[4,32,8,256]{3,2,1,0:T(8,128)(2,1)} %bitcast.18, bf16[128,8,8,128]{3,2,1,0:T(8,128)(2,1)} %bitcast.17, bf16[4,32,8,256]{3,2,1,0:T(8,128)(2,1)} %bitcast.19, s32[4,32]{1,0:T(4,128)S(1)} %pad_add_fusion.tabs), custom_call_target="tpu_custom_call" | custom-call | tf_op jit(solution)/shard_map/exchange/pallas_call | solution.py:333
  77.0 3.6 %place.1 = (bf16[2048,1024]{1,0:T(8,128)(2,1)}, bf16[128,8192]{1,0:T(8,128)(2,1)}) custom-call(bf16[32,224,128]{2,1,0:T(8,128)(2,1)S(1)} %get-tuple-element.6.got, bf16[128,8192]{1,0:T(8,128)(2,1)S(1)} %get-tuple-element.7.long_in), custom_call_target="tpu_custom_call" | custom-call | tf_op jit(solution)/shard_map/place/pallas_call | solution.py:403
  (2 shorter events, 0.0 us)
